TPU v7x, 32 devices: a whole 2x2x4 slice. The times are simulated.
32 devices in a mesh: gx: 8 (over y, x, core), gy: 4 (over z).
Axes of the slice: x: 2, y: 2, z: 4, core: 2. Of those that a mesh axis runs over, the one named last changes fastest.
Arguments:
- adjoint_source: float32 [4, 64, 256, 512], P(None, 'gx', 'gy'), may hold values from -40 to 40, as said below
- conductivity: float32 [64, 256, 512], P('gx', 'gy'), may hold values from 0.1 to 10
- electrodes: int32 [4], replicated, may hold values from 0 to 16383
Outputs:
- solution_field: float32 [4, 64, 256, 512], P(None, 'gx', 'gy')
- residual: float32 [4, 64, 256, 512], P(None, 'gx', 'gy')
Inputs may be any that keep to these rules, and one draw needn't show every extreme that they name: `electrodes`: each entry is a surface cell index, its first coordinate times 256 plus its second. `adjoint_source`: drawn afresh cell by cell.
All inputs are finite; a program needn't handle non-finite values.
Results may differ from a plain program's by a relative error of at most 0.0003.
Values sent between devices are 32-bit elements; how exact they have to be, the bound alone decides.
A program may use at most 128 MiB of HBM per device.

v0:
```python
import math

import jax
import jax.numpy as jnp
from jax import lax
from jax.sharding import PartitionSpec as P

ITERS = 2


def with_halo(block, sides, width):
    for axis, dim in sides:
        count = lax.axis_size(axis)
        forward = [(i, i + 1) for i in range(count - 1)]
        backward = [(target, source) for source, target in forward]
        low = lax.ppermute(
            lax.slice_in_dim(block, block.shape[dim] - width, None, axis=dim), axis, forward
        )
        high = lax.ppermute(lax.slice_in_dim(block, 0, width, axis=dim), axis, backward)
        block = jnp.concatenate([low, block, high], axis=dim)
    return block


def face_coefficients(padded):
    center = padded[1:-1, 1:-1, 1:-1]

    def face(neighbour):
        return jnp.where(neighbour > 0.0, 0.5 * (center + neighbour), center)

    return (
        face(padded[2:, 1:-1, 1:-1]),
        face(padded[:-2, 1:-1, 1:-1]),
        face(padded[1:-1, 2:, 1:-1]),
        face(padded[1:-1, :-2, 1:-1]),
        face(padded[1:-1, 1:-1, 2:]),
        face(padded[1:-1, 1:-1, :-2]),
    )


def apply_operator(rimmed, coeffs):
    padded = jnp.pad(rimmed, ((0, 0), (0, 0), (0, 0), (1, 1)))
    center = padded[:, 1:-1, 1:-1, 1:-1]
    others = (
        padded[:, 2:, 1:-1, 1:-1],
        padded[:, :-2, 1:-1, 1:-1],
        padded[:, 1:-1, 2:, 1:-1],
        padded[:, 1:-1, :-2, 1:-1],
        padded[:, 1:-1, 1:-1, 2:],
        padded[:, 1:-1, 1:-1, :-2],
    )
    total = jnp.zeros(center.shape, jnp.float32)
    for coeff, other in zip(coeffs, others):
        total = total + coeff[None] * (center - other)
    return total


def gram(left, right):
    return jnp.einsum("ixyz,jxyz->ij", left, right, precision=lax.Precision.HIGHEST)


def combine(matrix, block):
    return jnp.einsum("ij,ixyz->jxyz", matrix, block, precision=lax.Precision.HIGHEST)


def small_solve(spd, rhs):
    factor = jnp.linalg.cholesky(spd)
    return jax.scipy.linalg.cho_solve((factor, True), rhs)


def residual_image(residual, coeffs):
    rimmed = with_halo(residual, (("gx", 1), ("gy", 2)), 1)
    return apply_operator(rimmed, coeffs)


def paired_products(residual, image):
    return lax.psum((gram(residual, residual), gram(residual, image)), ("gx", "gy"))


def shards(adjoint_source, conductivity, electrodes):
    rim_sigma = with_halo(conductivity, (("gx", 0), ("gy", 1)), 1)
    coeffs = face_coefficients(jnp.pad(rim_sigma, ((0, 0), (0, 0), (1, 1))))
    cells_x = adjoint_source.shape[1]
    cells_y = adjoint_source.shape[2]
    cells_z = adjoint_source.shape[3]
    total_x = cells_x * lax.axis_size("gx")
    total_y = cells_y * lax.axis_size("gy")
    current = math.sqrt(total_x * total_y * cells_z)
    start_x = lax.axis_index("gx") * cells_x
    start_y = lax.axis_index("gy") * cells_y
    row_x = electrodes // total_y
    row_y = electrodes % total_y
    mark_x = ((start_x + jnp.arange(cells_x, dtype=jnp.int32))[None, :] == row_x[:, None]).astype(
        jnp.float32
    )
    mark_y = ((start_y + jnp.arange(cells_y, dtype=jnp.int32))[None, :] == row_y[:, None]).astype(
        jnp.float32
    )
    spike = current * (mark_x[:, :, None] * mark_y[:, None, :])
    right_side = adjoint_source.at[:, :, :, 0].add(spike)
    solution_field = jnp.zeros_like(right_side)
    residual = right_side
    direction = right_side
    image = residual_image(residual, coeffs)
    norm_now, curvature = paired_products(residual, image)
    along = image
    for step in range(ITERS):
        alpha = small_solve(curvature, norm_now)
        solution_field = solution_field + combine(alpha, direction)
        residual = residual - combine(alpha, along)
        if step + 1 < ITERS:
            image = residual_image(residual, coeffs)
            norm_next, cross = paired_products(residual, image)
            beta = small_solve(norm_now, norm_next)
            weighted = jnp.dot(curvature, beta, precision=lax.Precision.HIGHEST)
            curvature = cross - jnp.dot(beta.T, weighted, precision=lax.Precision.HIGHEST)
            direction = residual + combine(beta, direction)
            along = image + combine(beta, along)
            norm_now = norm_next
    return (solution_field, residual)


def solution(mesh):
    placed = (P(None, "gx", "gy", None), P("gx", "gy", None), P())
    return jax.shard_map(
        shards,
        mesh=mesh,
        in_specs=placed,
        out_specs=(P(None, "gx", "gy", None), P(None, "gx", "gy", None)),
        check_vma=False,
    )
```

profile of v0, /device:TPU:0, one launch (start us, length us, event | category | flops | bytes accessed | tf_op | source)
XLA Modules:
  0.0 339.9 jit_solution(11760287476002612887)
XLA Ops:
  0.6 1.0 fusion.70
  1.6 2.4 collective-permute-start.2
  4.0 1.3 collective-permute-start
  5.3 0.7 and_select_fusion.1
  6.2 4.9 %copy.25 = f32[4,8,64,512]{3,0,2,1:T(4,128)S(1)} copy(f32[4,8,64,512]{3,2,1,0:T(8,128)} %param.8) | data formatting | bytes 8388608 | tf_op args[0]
  11.2 1.9 copy-done.2
  13.1 0.3 slice_add_fusion
  13.4 8.9 %scatter-add.4 = f32[4,8,64,512]{3,0,2,1:T(4,128)} dynamic-update-slice(f32[4,8,64,512]{3,0,2,1:T(4,128)} %copy-done.2, f32[4,8,64,1]{3,0,2,1:T(4,128)S(1)} %slice_add_fusion, s32[]{:T(128)} %constant.100.clone.1, s32[]{:T(128)} %constant.100.clone.1, s32[]{:T(128)} %constant.100.clone.1, s32[]{:T(128)} %constant.100.clone.1) | dynamic-update-slice | bytes 16388 | tf_op jit(solution)/shard_map/scatter-add | solution.py:99
  22.3 1.4 fusion.68
  23.8 1.4 collective-permute-start.1
  25.2 5.8 %collective-permute-start.3 = (f32[4,1,64,512]{3,0,2,1:T(4,128)S(1)}, f32[4,1,64,512]{3,0,2,1:T(4,128)S(1)}, u32[]{:S(2)}, u32[]{:S(2)}) collective-permute-start(f32[4,1,64,512]{3,0,2,1:T(4,128)S(1)} %get-tuple-element.30), channel_id=1, source_target_pairs={{0,4},{4,8},{8,12},{12,16},{16,20},{20,24},{24,28},{1,5},{5,9},{9,... | collective-permute-start | bytes 1572872 | tf_op jit(solution)/shard_map/ppermute | solution.py:16
  31.0 0.3 fusion.45
  31.4 1.3 collective-permute-start.4
  32.7 4.8 %collective-permute-start.6 = (f32[10,1,512]{2,1,0:T(1,128)S(1)}, f32[10,1,512]{2,1,0:T(1,128)S(1)}, u32[]{:S(2)}, u32[]{:S(2)}) collective-permute-start(f32[10,1,512]{2,1,0:T(1,128)S(1)} %get-tuple-element.36), channel_id=1, source_target_pairs={{0,1},{1,2},{2,3},{4,5},{5,6},{6,7},{8,9},{9,10},{10,11},{12,13},{... | collective-permute-start | bytes 61448 | tf_op jit(solution)/shard_map/ppermute | solution.py:16
  37.5 18.0 %convolution_bitcast_fusion.4 = f32[4,4]{0,1:T(4,128)S(1)} fusion(f32[4,8,64,512]{3,0,2,1:T(4,128)S(1)} %copy-done.3), kind=kOutput, calls=%fused_computation.77 | convolution fusion | flops 50331648 | bytes 4194368 | tf_op jit(solution)/shard_map/ixyz,jxyz->ij/dot_general | solution.py:58
  55.5 0.7 select_maximum_fusion.8
  56.3 1.3 collective-permute-start.5
  57.6 5.0 %collective-permute-start.7 = (f32[4,10,1,512]{3,0,2,1:T(4,128)S(1)}, f32[4,10,1,512]{3,0,2,1:T(4,128)S(1)}, u32[]{:S(2)}, u32[]{:S(2)}) collective-permute-start(f32[4,10,1,512]{3,0,2,1:T(4,128)S(1)} %get-tuple-element.26), channel_id=1, source_target_pairs={{0,1},{1,2},{2,3},{4,5},{5,6},{6,7},{8,9},{9,10},{10,11},{12,13},{... | collective-permute-start | bytes 245768 | tf_op jit(solution)/shard_map/ppermute | solution.py:16
  62.6 1.0 multiply_select_fusion.3
  63.7 1.2 collective-permute-done.7
  64.9 11.7 %select_maximum_fusion.4 = f32[4,10,66,514]{3,0,2,1:T(4,128)S(1)} fusion(f32[4,10,1,512]{3,0,2,1:T(4,128)S(1)} %collective-permute-done.5, f32[4,10,1,512]{3,0,2,1:T(4,128)S(1)} %collective-permute-done.7, f32[4,1,64,512]{3,0,2,1:T(4,128)S(1)} %collective-permute-done.1, f32[4,8,64,512]{3,0,2,1:T(4,128)S(1)} %copy-done.3, ...), kind=kLoop, calls=%fused_computation.6 | loop fusion | flops 16283520 | bytes 10834560 | tf_op jit(solution)/shard_map/concatenate | solution.py:20
  76.7 10.1 %fusion.17 = f32[4,8,64,512]{3,0,2,1:T(4,128)S(1)} fusion(f32[4,8,64,512]{3,0,2,1:T(4,128)S(1)} %copy-done.3, f32[4,10,66,514]{3,0,2,1:T(4,128)S(1)} %select_maximum_fusion.4, f32[4,10,1,512]{3,0,2,1:T(4,128)S(1)} %collective-permute-done.7, f32[4,1,64,512]{3,0,2,1:T(4,128)S(1)} %collective-permute-done.1, f32[4,1,64,512]{3,0,2,1:T(4,128)S(1)} %collective-permute-done.3, ...), kind=kLoop, calls=%fused_computation.38 | loop fusion | flops 26214400 | bytes 24281088 | tf_op jit(solution)/shard_map/add | solution.py:53
  86.8 2.0 copy-done.6
  88.8 18.3 %convolution_bitcast_fusion.5 = f32[4,4]{0,1:T(4,128)S(1)} fusion(f32[4,8,64,512]{3,0,2,1:T(4,128)S(1)} %copy-done.3, f32[4,8,64,512]{3,0,2,1:T(4,128)S(1)} %fusion.17), kind=kOutput, calls=%fused_computation.78 | convolution fusion | flops 50331648 | bytes 8388672 | tf_op jit(solution)/shard_map/ixyz,jxyz->ij/dot_general | solution.py:58
  107.0 41.2 %all-reduce.4 = (f32[4,4]{0,1:T(4,128)S(1)}, f32[4,4]{0,1:T(4,128)S(1)}) all-reduce(f32[4,4]{0,1:T(4,128)S(1)} %convolution_bitcast_fusion.4, f32[4,4]{0,1:T(4,128)S(1)} %convolution_bitcast_fusion.5), channel_id=1, replica_groups=mesh['gx'=8,'gy'=4] {'gx','gy'}, use_global_device_ids=true, to_apply=%region_3.5 | all-reduce | flops 32 | bytes 256 | tf_op jit(solution)/shard_map/psum | solution.py:76
  148.5 0.4 cholesky.70
  148.8 0.7 compare_reduce_fusion.1
  149.5 0.4 cholesky.59
  149.9 0.6 compare_reduce_fusion.2
  150.5 0.5 fusion.47
  151.1 0.3 custom-call.9
  151.4 0.2 fusion.57
  151.6 0.2 convolution_bitcast_fusion.3
  151.8 10.1 %convolution_subtract_fusion = f32[4,8,64,512]{3,0,2,1:T(4,128)S(1)} fusion(f32[4,8,64,512]{3,0,2,1:T(4,128)} %scatter-add.4, f32[4,4,1,1]{0,1,3,2:T(4,128)S(1)} %convolution_bitcast_fusion.3, f32[4,8,64,512]{3,0,2,1:T(4,128)} %copy-done.6), kind=kOutput, calls=%fused_computation.67 | convolution fusion | flops 51380224 | bytes 12582976 | tf_op jit(solution)/shard_map/ij,ixyz->jxyz/dot_general | solution.py:62
  162.0 1.3 collective-permute-start.8
  163.3 3.2 collective-permute-start.9
  166.6 19.1 %convolution_bitcast_fusion.1 = f32[4,4]{1,0:T(4,128)S(1)} fusion(f32[4,8,64,512]{3,0,2,1:T(4,128)S(1)} %convolution_subtract_fusion), kind=kOutput, calls=%fused_computation.74 | convolution fusion | flops 50331648 | bytes 4194368 | tf_op jit(solution)/shard_map/ixyz,jxyz->ij/dot_general | solution.py:58
  185.8 1.3 collective-permute-start.10
  187.1 4.6 %collective-permute-start.11 = (f32[4,10,1,512]{3,0,2,1:T(4,128)S(1)}, f32[4,10,1,512]{3,0,2,1:T(4,128)S(1)}, u32[]{:S(2)}, u32[]{:S(2)}) collective-permute-start(f32[4,10,1,512]{3,0,2,1:T(4,128)S(1)} %get-tuple-element.24), channel_id=1, source_target_pairs={{0,1},{1,2},{2,3},{4,5},{5,6},{6,7},{8,9},{9,10},{10,11},{12,13},{... | collective-permute-start | bytes 245768 | tf_op jit(solution)/shard_map/ppermute | solution.py:16
  191.7 0.6 fusion.48
  192.3 1.5 collective-permute-done.11
  193.9 11.7 %select_maximum_fusion = f32[4,10,66,514]{3,0,2,1:T(4,128)S(1)} fusion(f32[4,10,1,512]{3,0,2,1:T(4,128)S(1)} %collective-permute-done.10, f32[4,10,1,512]{3,0,2,1:T(4,128)S(1)} %collective-permute-done.11, f32[4,1,64,512]{3,0,2,1:T(4,128)S(1)} %collective-permute-done.8, f32[4,8,64,512]{3,0,2,1:T(4,128)S(1)} %convolution_subtract_fusion, ...), kind=kLoop, calls=%fused_computation.2 | loop fusion | flops 16283520 | bytes 10834560 | tf_op jit(solution)/shard_map/concatenate | solution.py:20
  205.6 10.1 %fusion.2 = f32[4,8,64,512]{3,0,2,1:T(4,128)S(1)} fusion(f32[4,8,64,512]{3,0,2,1:T(4,128)S(1)} %convolution_subtract_fusion, f32[4,10,66,514]{3,0,2,1:T(4,128)S(1)} %select_maximum_fusion, f32[4,10,1,512]{3,0,2,1:T(4,128)S(1)} %collective-permute-done.11, f32[4,1,64,512]{3,0,2,1:T(4,128)S(1)} %collective-permute-done.8, ...), kind=kLoop, calls=%fused_computation.13 | loop fusion | flops 26214400 | bytes 24281088 | tf_op jit(solution)/shard_map/add | solution.py:53
  215.7 2.0 copy-done.7
  217.7 18.3 %convolution_bitcast_fusion.2 = f32[4,4]{0,1:T(4,128)S(1)} fusion(f32[4,8,64,512]{3,0,2,1:T(4,128)S(1)} %convolution_subtract_fusion, f32[4,8,64,512]{3,0,2,1:T(4,128)S(1)} %fusion.2), kind=kOutput, calls=%fused_computation.75 | convolution fusion | flops 50331648 | bytes 8388672 | tf_op jit(solution)/shard_map/ixyz,jxyz->ij/dot_general | solution.py:58
  236.0 0.3 custom-call.10
  236.3 42.1 %all-reduce.3 = (f32[4,4]{1,0:T(4,128)S(1)}, f32[4,4]{0,1:T(4,128)S(1)}) all-reduce(f32[4,4]{1,0:T(4,128)S(1)} %convolution_bitcast_fusion.1, f32[4,4]{0,1:T(4,128)S(1)} %convolution_bitcast_fusion.2), channel_id=1, replica_groups=mesh['gx'=8,'gy'=4] {'gx','gy'}, use_global_device_ids=true, to_apply=%region_5.8 | all-reduce | flops 32 | bytes 256 | tf_op jit(solution)/shard_map/psum | solution.py:76
  278.4 0.2 fusion.53
  278.8 11.5 %fusion.60 = f32[4,8,64,512]{3,0,2,1:T(4,128)} fusion(f32[4,8,64,512]{3,0,2,1:T(4,128)} %copy-done.6, f32[4,4]{1,0:T(4,128)S(1)} %fusion.55), kind=kOutput, calls=%fused_computation.122 | convolution fusion | flops 50331648 | bytes 8388672 | tf_op jit(solution)/shard_map/ij,ixyz->jxyz/dot_general | solution.py:62
  290.2 0.2 fusion.72
  290.4 10.3 %fusion.62 = f32[4,8,64,512]{3,0,2,1:T(4,128)} fusion(f32[4,8,64,512]{3,0,2,1:T(4,128)S(1)} %copy-done.4, f32[4,4]{1,0:T(4,128)S(1)} %fusion.55), kind=kOutput, calls=%fused_computation.124 | convolution fusion | flops 50331648 | bytes 8388672 | tf_op jit(solution)/shard_map/ij,ixyz->jxyz/dot_general | solution.py:62
  300.7 0.2 fusion.71
  301.0 0.4 cholesky.81
  301.4 0.6 compare_reduce_fusion
  302.1 0.6 fusion.49
  302.7 0.3 custom-call.11
  303.1 0.2 fusion.50
  303.3 0.2 convolution_bitcast_fusion
  303.5 11.4 %fusion.36 = f32[4,8,64,512]{3,0,2,1:T(4,128)S(1)} fusion(f32[4,8,64,512]{3,0,2,1:T(4,128)} %copy-done, f32[4,4,1,1]{0,1,3,2:T(4,128)S(1)} %convolution_bitcast_fusion, f32[4,8,64,512]{3,0,2,1:T(4,128)} %copy-done.7, f32[4,8,64,512]{3,0,2,1:T(4,128)} %fusion.60), kind=kOutput, calls=%fused_computation.72 | convolution fusion | flops 52428800 | bytes 16777280 | tf_op jit(solution)/shard_map/ij,ixyz->jxyz/dot_general | solution.py:62
  314.9 3.4 %copy.41 = f32[4,8,64,512]{3,2,1,0:T(8,128)} copy(f32[4,8,64,512]{3,0,2,1:T(4,128)S(1)} %fusion.36) | data formatting | bytes 8388608
  318.3 1.5 copy-done.8
  319.9 8.1 %fusion.33 = f32[4,8,64,512]{3,0,2,1:T(4,128)S(1)} fusion(f32[4,4,1,1]{0,1,3,2:T(4,128)S(1)} %convolution_bitcast_fusion, f32[4,8,64,512]{3,0,2,1:T(4,128)S(1)} %copy-done.1, f32[4,8,64,512]{3,0,2,1:T(4,128)S(1)} %copy-done.8), kind=kOutput, calls=%fused_computation.63 | convolution fusion | flops 51380224 | bytes 12582976 | tf_op jit(solution)/shard_map/ij,ixyz->jxyz/dot_general | solution.py:62
  328.0 8.4 %convolution_add_fusion = f32[4,8,64,512]{3,0,2,1:T(4,128)S(1)} fusion(f32[4,8,64,512]{3,0,2,1:T(4,128)S(1)} %fusion.33, f32[4,4,1,1]{0,1,3,2:T(4,128)S(1)} %convolution_bitcast_fusion.3, f32[4,8,64,512]{3,0,2,1:T(4,128)S(1)} %copy-done.5), kind=kOutput, calls=%fused_computation.68 | convolution fusion | flops 51380224 | bytes 12582976 | tf_op jit(solution)/shard_map/ij,ixyz->jxyz/dot_general | solution.py:62
  336.4 3.3 copy.40
  (60 shorter events, 1.1 us)
Async XLA Ops:
  1.6 29.4 %collective-permute-start.2 = (f32[1,64,512]{2,1,0:T(8,128)S(1)}, f32[1,64,512]{2,1,0:T(8,128)S(1)}, u32[]{:S(2)}, u32[]{:S(2)}) collective-permute-start(f32[1,64,512]{2,1,0:T(8,128)S(1)} %get-tuple-element.44), channel_id=1, source_target_pairs={{0,4},{4,8},{8,12},{12,16},{16,20},{20,24},{24,28},{1,5},{5,9},{9,... | collective-permute-start | bytes 393224 | tf_op jit(solution)/shard_map/ppermute | solution.py:16
  4.0 27.0 %collective-permute-start = (f32[1,64,512]{2,1,0:T(8,128)S(1)}, f32[1,64,512]{2,1,0:T(8,128)S(1)}, u32[]{:S(2)}, u32[]{:S(2)}) collective-permute-start(f32[1,64,512]{2,1,0:T(8,128)S(1)} %get-tuple-element.43), channel_id=1, source_target_pairs={{4,0},{8,4},{12,8},{16,12},{20,16},{24,20},{28,24},{5,1},{9,5},{13... | collective-permute-start | bytes 393224 | tf_op jit(solution)/shard_map/ppermute | solution.py:19
  11.1 2.0 copy-start.2
  11.1 19.9 %copy-start.15 = (f32[8,64,512]{2,1,0:T(8,128)S(1)}, f32[8,64,512]{2,1,0:T(8,128)}, u32[]{:S(2)}) copy-start(f32[8,64,512]{2,1,0:T(8,128)} %param.9) | copy-start | bytes 3145732
  22.3 15.2 %copy-start.3 = (f32[4,8,64,512]{3,0,2,1:T(4,128)S(1)}, f32[4,8,64,512]{3,0,2,1:T(4,128)}, u32[]{:S(2)}) copy-start(f32[4,8,64,512]{3,0,2,1:T(4,128)} %scatter-add.4) | copy-start | bytes 12582916
  23.8 32.5 %collective-permute-start.1 = (f32[4,1,64,512]{3,0,2,1:T(4,128)S(1)}, f32[4,1,64,512]{3,0,2,1:T(4,128)S(1)}, u32[]{:S(2)}, u32[]{:S(2)}) collective-permute-start(f32[4,1,64,512]{3,0,2,1:T(4,128)S(1)} %get-tuple-element.31), channel_id=1, source_target_pairs={{4,0},{8,4},{12,8},{16,12},{20,16},{24,20},{28,24},{5,1},{9,5},{13... | collective-permute-start | bytes 1572872 | tf_op jit(solution)/shard_map/ppermute | solution.py:19
  25.2 31.1 %collective-permute-start.3 = (f32[4,1,64,512]{3,0,2,1:T(4,128)S(1)}, f32[4,1,64,512]{3,0,2,1:T(4,128)S(1)}, u32[]{:S(2)}, u32[]{:S(2)}) collective-permute-start(f32[4,1,64,512]{3,0,2,1:T(4,128)S(1)} %get-tuple-element.30), channel_id=1, source_target_pairs={{0,4},{4,8},{8,12},{12,16},{16,20},{20,24},{24,28},{1,5},{5,9},{9,... | collective-permute-start | bytes 1572872 | tf_op jit(solution)/shard_map/ppermute | solution.py:16
  31.4 24.1 %collective-permute-start.4 = (f32[10,1,512]{2,1,0:T(1,128)S(1)}, f32[10,1,512]{2,1,0:T(1,128)S(1)}, u32[]{:S(2)}, u32[]{:S(2)}) collective-permute-start(f32[10,1,512]{2,1,0:T(1,128)S(1)} %get-tuple-element.37), channel_id=1, source_target_pairs={{1,0},{2,1},{3,2},{5,4},{6,5},{7,6},{9,8},{10,9},{11,10},{13,12},{... | collective-permute-start | bytes 61448 | tf_op jit(solution)/shard_map/ppermute | solution.py:19
  32.7 22.8 %collective-permute-start.6 = (f32[10,1,512]{2,1,0:T(1,128)S(1)}, f32[10,1,512]{2,1,0:T(1,128)S(1)}, u32[]{:S(2)}, u32[]{:S(2)}) collective-permute-start(f32[10,1,512]{2,1,0:T(1,128)S(1)} %get-tuple-element.36), channel_id=1, source_target_pairs={{0,1},{1,2},{2,3},{4,5},{5,6},{6,7},{8,9},{9,10},{10,11},{12,13},{... | collective-permute-start | bytes 61448 | tf_op jit(solution)/shard_map/ppermute | solution.py:16
  55.5 7.2 %copy-start.16 = (f32[8,64,512]{2,1,0:T(8,128)S(1)}, f32[8,64,512]{2,1,0:T(8,128)}, u32[]{:S(2)}) copy-start(f32[8,64,512]{2,1,0:T(8,128)} %param.9) | copy-start | bytes 3145732
  56.3 7.4 %collective-permute-start.5 = (f32[4,10,1,512]{3,0,2,1:T(4,128)S(1)}, f32[4,10,1,512]{3,0,2,1:T(4,128)S(1)}, u32[]{:S(2)}, u32[]{:S(2)}) collective-permute-start(f32[4,10,1,512]{3,0,2,1:T(4,128)S(1)} %get-tuple-element.27), channel_id=1, source_target_pairs={{1,0},{2,1},{3,2},{5,4},{6,5},{7,6},{9,8},{10,9},{11,10},{13,12},{... | collective-permute-start | bytes 245768 | tf_op jit(solution)/shard_map/ppermute | solution.py:19
  57.6 7.3 %collective-permute-start.7 = (f32[4,10,1,512]{3,0,2,1:T(4,128)S(1)}, f32[4,10,1,512]{3,0,2,1:T(4,128)S(1)}, u32[]{:S(2)}, u32[]{:S(2)}) collective-permute-start(f32[4,10,1,512]{3,0,2,1:T(4,128)S(1)} %get-tuple-element.26), channel_id=1, source_target_pairs={{0,1},{1,2},{2,3},{4,5},{5,6},{6,7},{8,9},{9,10},{10,11},{12,13},{... | collective-permute-start | bytes 245768 | tf_op jit(solution)/shard_map/ppermute | solution.py:16
  63.7 13.0 %copy-start.9 = (f32[8,64,512]{2,1,0:T(8,128)}, f32[8,64,512]{2,1,0:T(8,128)S(1)}, u32[]{:S(2)}) copy-start(f32[8,64,512]{2,1,0:T(8,128)S(1)} %get-tuple-element.35) | copy-start | bytes 3145732
  63.7 13.0 %copy-start.11 = (f32[8,64,512]{2,1,0:T(8,128)}, f32[8,64,512]{2,1,0:T(8,128)S(1)}, u32[]{:S(2)}) copy-start(f32[8,64,512]{2,1,0:T(8,128)S(1)} %get-tuple-element.41) | copy-start | bytes 3145732
  63.7 13.0 %copy-start.13 = (f32[8,64,512]{2,1,0:T(8,128)}, f32[8,64,512]{2,1,0:T(8,128)S(1)}, u32[]{:S(2)}) copy-start(f32[8,64,512]{2,1,0:T(8,128)S(1)} %get-tuple-element.42) | copy-start | bytes 3145732
  86.8 2.0 copy-start.6
  161.9 53.8 %copy-start = (f32[4,8,64,512]{3,0,2,1:T(4,128)}, f32[4,8,64,512]{3,0,2,1:T(4,128)S(1)}, u32[]{:S(2)}) copy-start(f32[4,8,64,512]{3,0,2,1:T(4,128)S(1)} %convolution_subtract_fusion) | copy-start | bytes 12582916
  162.0 23.7 %collective-permute-start.8 = (f32[4,1,64,512]{3,0,2,1:T(4,128)S(1)}, f32[4,1,64,512]{3,0,2,1:T(4,128)S(1)}, u32[]{:S(2)}, u32[]{:S(2)}) collective-permute-start(f32[4,1,64,512]{3,0,2,1:T(4,128)S(1)} %get-tuple-element.29), channel_id=1, source_target_pairs={{4,0},{8,4},{12,8},{16,12},{20,16},{24,20},{28,24},{5,1},{9,5},{13... | collective-permute-start | bytes 1572872 | tf_op jit(solution)/shard_map/ppermute | solution.py:19
  163.3 22.4 %collective-permute-start.9 = (f32[4,1,64,512]{3,0,2,1:T(4,128)S(1)}, f32[4,1,64,512]{3,0,2,1:T(4,128)S(1)}, u32[]{:S(2)}, u32[]{:S(2)}) collective-permute-start(f32[4,1,64,512]{3,0,2,1:T(4,128)S(1)} %get-tuple-element.28), channel_id=1, source_target_pairs={{0,4},{4,8},{8,12},{12,16},{16,20},{20,24},{24,28},{1,5},{5,9},{9,... | collective-permute-start | bytes 1572872 | tf_op jit(solution)/shard_map/ppermute | solution.py:16
  185.8 6.5 %collective-permute-start.10 = (f32[4,10,1,512]{3,0,2,1:T(4,128)S(1)}, f32[4,10,1,512]{3,0,2,1:T(4,128)S(1)}, u32[]{:S(2)}, u32[]{:S(2)}) collective-permute-start(f32[4,10,1,512]{3,0,2,1:T(4,128)S(1)} %get-tuple-element.25), channel_id=1, source_target_pairs={{1,0},{2,1},{3,2},{5,4},{6,5},{7,6},{9,8},{10,9},{11,10},{13,12},{... | collective-permute-start | bytes 245768 | tf_op jit(solution)/shard_map/ppermute | solution.py:19
  187.1 6.8 %collective-permute-start.11 = (f32[4,10,1,512]{3,0,2,1:T(4,128)S(1)}, f32[4,10,1,512]{3,0,2,1:T(4,128)S(1)}, u32[]{:S(2)}, u32[]{:S(2)}) collective-permute-start(f32[4,10,1,512]{3,0,2,1:T(4,128)S(1)} %get-tuple-element.24), channel_id=1, source_target_pairs={{0,1},{1,2},{2,3},{4,5},{5,6},{6,7},{8,9},{9,10},{10,11},{12,13},{... | collective-permute-start | bytes 245768 | tf_op jit(solution)/shard_map/ppermute | solution.py:16
  192.3 13.3 %copy-start.10 = (f32[8,64,512]{2,1,0:T(8,128)S(1)}, f32[8,64,512]{2,1,0:T(8,128)}, u32[]{:S(2)}) copy-start(f32[8,64,512]{2,1,0:T(8,128)} %copy-done.9) | copy-start | bytes 3145732
  192.3 13.3 %copy-start.12 = (f32[8,64,512]{2,1,0:T(8,128)S(1)}, f32[8,64,512]{2,1,0:T(8,128)}, u32[]{:S(2)}) copy-start(f32[8,64,512]{2,1,0:T(8,128)} %copy-done.11) | copy-start | bytes 3145732
  192.3 13.3 %copy-start.14 = (f32[8,64,512]{2,1,0:T(8,128)S(1)}, f32[8,64,512]{2,1,0:T(8,128)}, u32[]{:S(2)}) copy-start(f32[8,64,512]{2,1,0:T(8,128)} %copy-done.13) | copy-start | bytes 3145732
  215.7 2.0 copy-start.7
  278.8 11.7 %copy-start.4 = (f32[4,8,64,512]{3,0,2,1:T(4,128)S(1)}, f32[4,8,64,512]{3,0,2,1:T(4,128)}, u32[]{:S(2)}) copy-start(f32[4,8,64,512]{3,0,2,1:T(4,128)} %scatter-add.4) | copy-start | bytes 12582916
  314.9 3.4 %copy-start.1 = (f32[4,8,64,512]{3,0,2,1:T(4,128)S(1)}, f32[4,8,64,512]{3,0,2,1:T(4,128)}, u32[]{:S(2)}) copy-start(f32[4,8,64,512]{3,0,2,1:T(4,128)} %copy-done) | copy-start | bytes 12582916
  314.9 5.0 %copy-start.8 = (f32[4,8,64,512]{3,0,2,1:T(4,128)S(1)}, f32[4,8,64,512]{3,0,2,1:T(4,128)}, u32[]{:S(2)}) copy-start(f32[4,8,64,512]{3,0,2,1:T(4,128)} %fusion.62) | copy-start | bytes 12582916
  319.9 8.1 %copy-start.5 = (f32[4,8,64,512]{3,0,2,1:T(4,128)S(1)}, f32[4,8,64,512]{3,0,2,1:T(4,128)}, u32[]{:S(2)}) copy-start(f32[4,8,64,512]{3,0,2,1:T(4,128)} %scatter-add.4) | copy-start | bytes 12582916
where the time goes:
time: 345 us; the launch traced here: 340 us
  matrix products  135 us (39%)
  blocking collectives  83.3 us (24%)
  other arithmetic  52.9 us (15%)
  starting transfers between devices  33.6 us (10%)
  local copies, waits for them, and re-layouts  30.9 us (9%)
    psum x2, blocking collectives, paired_products(): lax.psum((gram(residual, residual), gram(residual, image)), ('gx', 'gy'))  83.3 us
    dot_general x4, matrix products, gram(): jnp.einsum('ixyz,jxyz->ij', left, right, precision=lax.Precision.HIGHEST)  73.6 us
    dot_general x6, matrix products, combine(): jnp.einsum('ij,ixyz->jxyz', matrix, block, precision=lax.Precision.HIGHEST)  59.8 us
    ppermute x6, starting transfers between devices, with_halo(): lax.ppermute(lax.slice_in_dim(block, block.shape[dim] - width, None, axis...  25.8 us
    concatenate x5, other arithmetic, with_halo(): block = jnp.concatenate([low, block, high], axis=dim)  24.3 us
    add x2, other arithmetic, apply_operator(): total = total + coeff[None] * (center - other)  20.2 us
    unnamed x38, local copies, waits for them, and re-layouts  19.1 us
    scatter-add x1, local copies, waits for them, and re-layouts, shards(): right_side = adjoint_source.at[:, :, :, 0].add(spike)  8.89 us
  transfers between devices with their start and end apart: 12, of which 2 were waited for; matrix products, arithmetic and copies ran while one was open for 17% of the time, Pallas kernels for 0%

commit v1 on v0

v1 whole, which is shorter than its diff:
```python
import functools
import math

import jax
import jax.numpy as jnp
from jax import lax
from jax.experimental import pallas as pl
from jax.experimental.pallas import tpu as pltpu
from jax.sharding import PartitionSpec as P

MESH = pl.DeviceIdType.MESH
F = 4
PAIRS = [(i, j) for i in range(F) for j in range(i, F)]
NP = len(PAIRS)
TILE = 8
LANES = 128


def remote(src, dst, send, recv, axis, index):
    return pltpu.make_async_remote_copy(
        src_ref=src, dst_ref=dst, send_sem=send, recv_sem=recv,
        device_id={axis: index}, device_id_type=MESH,
    )


def operator_kernel(
    nx, ny, current, adj, sig, elec, r_out, q_out, w_out, sums,
    R, Q, W, S, wt, edge, got, acc, part_x, part_y,
    local, xs, xr, ys, yr, ax_s, ax_r, ay_s, ay_r,
):
    cx, cy, cz = sig.shape
    total_y = ny * cy
    mx, my = lax.axis_index("gx"), lax.axis_index("gy")
    barrier = pltpu.get_barrier_semaphore()
    rows = pl.ds(TILE, cy)

    load_r = pltpu.make_async_copy(adj, R.at[:, pl.ds(1, cx), rows, :], local.at[0])
    load_s = pltpu.make_async_copy(sig, S.at[pl.ds(1, cx), rows, :], local.at[1])
    load_r.start()
    load_s.start()
    for axis, me, n in (("gx", mx, nx), ("gy", my, ny)):
        for d in range(1, n):
            pl.semaphore_signal(
                barrier, inc=1, device_id={axis: lax.rem(me + d, n)}, device_id_type=MESH
            )
    pl.semaphore_wait(barrier, nx + ny - 2)

    has_lo, has_hi = mx > 0, mx < nx - 1
    below, above = jnp.maximum(mx - 1, 0), jnp.minimum(mx + 1, nx - 1)
    y_lo, y_hi = my > 0, my < ny - 1
    left, right = jnp.maximum(my - 1, 0), jnp.minimum(my + 1, ny - 1)

    up_s = remote(sig.at[cx - 1], S.at[0, rows, :], xs.at[0], xr.at[0], "gx", above)
    dn_s = remote(sig.at[0], S.at[cx + 1, rows, :], xs.at[1], xr.at[1], "gx", below)
    up_r = remote(adj.at[:, cx - 1], R.at[:, 0, rows, :], xs.at[2], xr.at[2], "gx", above)
    dn_r = remote(adj.at[:, 0], R.at[:, cx + 1, rows, :], xs.at[3], xr.at[3], "gx", below)
    up_q = remote(Q.at[:, cx, rows, :], Q.at[:, 0, rows, :], xs.at[4], xr.at[4], "gx", above)
    dn_q = remote(Q.at[:, 1, rows, :], Q.at[:, cx + 1, rows, :], xs.at[5], xr.at[5], "gx", below)
    y_up = remote(edge.at[0], got.at[0], ys.at[0], yr.at[0], "gy", right)
    y_dn = remote(edge.at[1], got.at[1], ys.at[1], yr.at[1], "gy", left)
    y_up_q = remote(edge.at[2, pl.ds(0, F)], got.at[2, pl.ds(0, F)], ys.at[2], yr.at[2], "gy", right)
    y_dn_q = remote(edge.at[3, pl.ds(0, F)], got.at[3, pl.ds(0, F)], ys.at[3], yr.at[3], "gy", left)

    @pl.when(has_hi)
    def _():
        up_s.start()
        up_r.start()

    @pl.when(has_lo)
    def _():
        dn_s.start()
        dn_r.start()

    acc[...] = jnp.zeros_like(acc)
    edge_plane = jnp.zeros((cy, cz), jnp.float32)

    @pl.when(jnp.logical_not(has_lo))
    def _():
        S[0, rows, :] = edge_plane
        for f in range(F):
            R[f, 0, rows, :] = edge_plane
            Q[f, 0, rows, :] = edge_plane

    @pl.when(jnp.logical_not(has_hi))
    def _():
        S[cx + 1, rows, :] = edge_plane
        for f in range(F):
            R[f, cx + 1, rows, :] = edge_plane
            Q[f, cx + 1, rows, :] = edge_plane

    @pl.when(jnp.logical_not(y_lo))
    def _():
        got[0] = jnp.zeros(got.shape[1:], jnp.float32)
        got[2] = jnp.zeros(got.shape[1:], jnp.float32)

    @pl.when(jnp.logical_not(y_hi))
    def _():
        got[1] = jnp.zeros(got.shape[1:], jnp.float32)
        got[3] = jnp.zeros(got.shape[1:], jnp.float32)

    row_id = lax.broadcasted_iota(jnp.int32, (cy, LANES), 0)
    first = lax.broadcasted_iota(jnp.int32, (cy, LANES), 1) == 0

    def spike(x):
        cell = row_id + ((mx * cx + x - 1) * total_y + my * cy)
        for f in range(F):
            here = jnp.where(first & (cell == elec[f]), current, 0.0)
            R[f, x, rows, pl.ds(0, LANES)] = R[f, x, rows, pl.ds(0, LANES)] + here

    def pack(src, fields, base):
        def one(x, c):
            for k, ref in enumerate(src(x)):
                edge[base, k, pl.ds(x, 1), :] = ref(TILE + cy - 1)
                edge[base + 1, k, pl.ds(x, 1), :] = ref(TILE)
            return c
        lax.fori_loop(0, cx, one, 0)

    def row_r(f, x):
        return lambda y: R[f, x + 1, pl.ds(y, 1), :]

    def row_q(f, x):
        return lambda y: Q[f, x + 1, pl.ds(y, 1), :]

    def row_s(x):
        return lambda y: S[x + 1, pl.ds(y, 1), :]

    load_r.wait()

    def spike_loop(x, c):
        spike(x)
        return c

    lax.fori_loop(1, cx + 1, spike_loop, 0)
    load_s.wait()
    pack(lambda x: [row_r(f, x) for f in range(F)] + [row_s(x)], F + 1, 0)

    @pl.when(y_hi)
    def _():
        y_up.start()

    @pl.when(y_lo)
    def _():
        y_dn.start()

    keep_r = pltpu.make_async_copy(R.at[:, pl.ds(1, cx), rows, :], r_out, local.at[2])
    keep_r.start()

    @pl.when(y_lo)
    def _():
        y_up.wait_recv()

    @pl.when(y_hi)
    def _():
        y_dn.wait_recv()

    def unpack_first(x, c):
        for slot, y in ((0, TILE - 1), (1, TILE + cy)):
            for f in range(F):
                R[f, x + 1, pl.ds(y, 1), :] = got[slot, f, pl.ds(x, 1), :]
            S[x + 1, pl.ds(y, 1), :] = got[slot, F, pl.ds(x, 1), :]
        return c

    lax.fori_loop(0, cx, unpack_first, 0)

    lane = lax.broadcasted_iota(jnp.int32, (TILE, cz), 1)

    def add_grams(base, lefts, rights):
        for k, (i, j) in enumerate(PAIRS):
            prod = lefts[i] * rights[j]
            total = prod[:, :LANES]
            for c in range(LANES, cz, LANES):
                total = total + prod[:, c:c + LANES]
            acc[base + k] = acc[base + k] + total

    def apply(src, f, x, y, weights):
        mid = src[f, x, pl.ds(y, TILE), :]
        diag, xm, xp, ym, yp, zm, zp = weights
        out = diag * mid
        out = out - xm * src[f, x - 1, pl.ds(y, TILE), :]
        out = out - xp * src[f, x + 1, pl.ds(y, TILE), :]
        out = out - ym * src[f, x, pl.ds(y - 1, TILE), :]
        out = out - yp * src[f, x, pl.ds(y + 1, TILE), :]
        out = out - zm * pltpu.roll(mid, 1, axis=1)
        out = out - zp * pltpu.roll(mid, cz - 1, axis=1)
        return mid, out

    def first_plane(x):
        for t in range(cy // TILE):
            y = TILE + t * TILE
            here = S[x, pl.ds(y, TILE), :]
            others = (
                S[x - 1, pl.ds(y, TILE), :],
                S[x + 1, pl.ds(y, TILE), :],
                S[x, pl.ds(y - 1, TILE), :],
                S[x, pl.ds(y + 1, TILE), :],
                jnp.where(lane == 0, 0.0, pltpu.roll(here, 1, axis=1)),
                jnp.where(lane == cz - 1, 0.0, pltpu.roll(here, cz - 1, axis=1)),
            )
            diag = jnp.zeros_like(here)
            weights = []
            for other in others:
                inside = other > 0.0
                mean = 0.5 * (here + other)
                diag = diag + jnp.where(inside, mean, here)
                weights.append(jnp.where(inside, mean, 0.0))
            weights = [diag] + weights
            for k in range(7):
                wt[k, x - 1, pl.ds(t * TILE, TILE), :] = weights[k]
            rs, qs = [], []
            for f in range(F):
                mid, out = apply(R, f, x, y, weights)
                Q[f, x, pl.ds(y, TILE), :] = out
                rs.append(mid)
                qs.append(out)
            add_grams(0, rs, rs)
            add_grams(NP, rs, qs)

    def second_plane(x):
        for t in range(cy // TILE):
            y = TILE + t * TILE
            weights = [wt[k, x - 1, pl.ds(t * TILE, TILE), :] for k in range(7)]
            qs, ws = [], []
            for f in range(F):
                mid, out = apply(Q, f, x, y, weights)
                W[f, x - 1, pl.ds(t * TILE, TILE), :] = out
                qs.append(mid)
                ws.append(out)
            add_grams(2 * NP, qs, qs)
            add_grams(3 * NP, qs, ws)

    def run(plane):
        def one(x, c):
            plane(x)
            return c
        return one

    lax.fori_loop(2, cx, run(first_plane), 0)

    @pl.when(has_lo)
    def _():
        up_s.wait_recv()
        up_r.wait_recv()

    @pl.when(has_hi)
    def _():
        dn_s.wait_recv()
        dn_r.wait_recv()

    def ends(plane):
        def one(k, c):
            plane(k)
            return c
        return one

    lax.fori_loop(0, 2, ends(lambda k: spike(k * (cx + 1))), 0)
    lax.fori_loop(0, 2, ends(lambda k: first_plane(1 + k * (cx - 1))), 0)

    @pl.when(has_hi)
    def _():
        up_q.start()

    @pl.when(has_lo)
    def _():
        dn_q.start()

    pack(lambda x: [row_q(f, x) for f in range(F)], F, 2)

    @pl.when(y_hi)
    def _():
        y_up_q.start()

    @pl.when(y_lo)
    def _():
        y_dn_q.start()

    keep_q = pltpu.make_async_copy(Q.at[:, pl.ds(1, cx), rows, :], q_out, local.at[3])
    keep_q.start()

    @pl.when(y_lo)
    def _():
        y_up_q.wait_recv()

    @pl.when(y_hi)
    def _():
        y_dn_q.wait_recv()

    def unpack_second(x, c):
        for slot, y in ((2, TILE - 1), (3, TILE + cy)):
            for f in range(F):
                Q[f, x + 1, pl.ds(y, 1), :] = got[slot, f, pl.ds(x, 1), :]
        return c

    lax.fori_loop(0, cx, unpack_second, 0)
    lax.fori_loop(2, cx, run(second_plane), 0)

    @pl.when(has_lo)
    def _():
        up_q.wait_recv()

    @pl.when(has_hi)
    def _():
        dn_q.wait_recv()

    lax.fori_loop(0, 2, ends(lambda k: second_plane(1 + k * (cx - 1))), 0)
    keep_w = pltpu.make_async_copy(W, w_out, local.at[4])
    keep_w.start()

    part_x[mx] = jnp.sum(acc[...], axis=1)

    def exchange(buf, axis, me, n, sends, recvs):
        copies = [
            remote(buf.at[me], buf.at[me], sends.at[d - 1], recvs.at[d - 1], axis, lax.rem(me + d, n))
            for d in range(1, n)
        ]
        for copy in copies:
            copy.start()
        for d in range(1, n):
            src = lax.rem(me + n - d, n)
            remote(
                buf.at[me], buf.at[src], sends.at[d - 1], recvs.at[d - 1], axis, src
            ).wait_recv()
        total = buf[0]
        for k in range(1, n):
            total = total + buf[k]
        return copies, total

    copies_x, total_x = exchange(part_x, "gx", mx, nx, ax_s, ax_r)
    part_y[my] = total_x
    copies_y, total = exchange(part_y, "gy", my, ny, ay_s, ay_r)
    sums[...] = jnp.broadcast_to(jnp.sum(total, axis=1, keepdims=True), sums.shape)

    for copy in copies_x + copies_y:
        copy.wait_send()

    @pl.when(has_hi)
    def _():
        up_s.wait_send()
        up_r.wait_send()
        up_q.wait_send()

    @pl.when(has_lo)
    def _():
        dn_s.wait_send()
        dn_r.wait_send()
        dn_q.wait_send()

    @pl.when(y_hi)
    def _():
        y_up.wait_send()
        y_up_q.wait_send()

    @pl.when(y_lo)
    def _():
        y_dn.wait_send()
        y_dn_q.wait_send()

    keep_r.wait()
    keep_q.wait()
    keep_w.wait()


def mat(a, b):
    return [
        [sum(a[i][k] * b[k][j] for k in range(1, F)) + a[i][0] * b[0][j] for j in range(F)]
        for i in range(F)
    ]


def add(a, b):
    return [[a[i][j] + b[i][j] for j in range(F)] for i in range(F)]


def sub(a, b):
    return [[a[i][j] - b[i][j] for j in range(F)] for i in range(F)]


def turn(a):
    return [[a[j][i] for j in range(F)] for i in range(F)]


def spd_solve(a, b):
    low = [[None] * F for _ in range(F)]
    inv = [None] * F
    rest = [list(row) for row in a]
    for k in range(F):
        inv[k] = 1.0 / rest[k][k]
        for i in range(k + 1, F):
            low[i][k] = rest[i][k] * inv[k]
        for i in range(k + 1, F):
            for j in range(k + 1, i + 1):
                rest[i][j] = rest[i][j] - low[i][k] * rest[j][k]
    out = [list(row) for row in b]
    for i in range(F):
        for k in range(i):
            out[i] = [u - low[i][k] * v for u, v in zip(out[i], out[k])]
    out = [[u * inv[i] for u in out[i]] for i in range(F)]
    for i in reversed(range(F)):
        for k in range(i + 1, F):
            out[i] = [u - low[k][i] * v for u, v in zip(out[i], out[k])]
    return out


def finish_kernel(sums, r_ref, q_ref, w_ref, x_ref, e_ref, coef):
    @pl.when(pl.program_id(0) == 0)
    def _():
        grams = []
        for g in range(4):
            m = [[None] * F for _ in range(F)]
            for k, (i, j) in enumerate(PAIRS):
                m[i][j] = m[j][i] = sums[pl.ds(g * NP + k, 1), :]
            grams.append(m)
        s0, s1, s2, s3 = grams
        a0 = spd_solve(s1, s0)
        s1a, s2a = mat(s1, a0), mat(s2, a0)
        a0t = turn(a0)
        rr = add(sub(sub(s0, s1a), turn(s1a)), mat(a0t, s2a))
        cross = add(sub(sub(s1, s2a), turn(s2a)), mat(a0t, mat(s3, a0)))
        beta = spd_solve(s0, rr)
        curve = sub(cross, mat(turn(beta), mat(s1, beta)))
        a1 = spd_solve(curve, rr)
        m1 = add(add(a0, a1), mat(beta, a1))
        m2 = mat(a0, a1)
        for i in range(F):
            for j in range(F):
                coef[pl.ds(i * F + j, 1), :] = m1[i][j]
                coef[pl.ds(F * F + i * F + j, 1), :] = m2[i][j]

    cy, cz = r_ref.shape[2:]
    c1 = [[jnp.broadcast_to(coef[pl.ds(i * F + j, 1), :], (TILE, LANES)) for j in range(F)] for i in range(F)]
    c2 = [[jnp.broadcast_to(coef[pl.ds(F * F + i * F + j, 1), :], (TILE, LANES)) for j in range(F)] for i in range(F)]

    def tile(t, c):
        y = pl.ds(pl.multiple_of(t * TILE, TILE), TILE)
        for z in range(0, cz, LANES):
            at = pl.ds(z, LANES)
            rs = [r_ref[f, 0, y, at] for f in range(F)]
            qs = [q_ref[f, 0, y, at] for f in range(F)]
            ws = [w_ref[f, 0, y, at] for f in range(F)]
            for j in range(F):
                field = rs[0] * c1[0][j] - qs[0] * c2[0][j]
                left = rs[j] - qs[0] * c1[0][j] + ws[0] * c2[0][j]
                for i in range(1, F):
                    field = field + rs[i] * c1[i][j] - qs[i] * c2[i][j]
                    left = left - qs[i] * c1[i][j] + ws[i] * c2[i][j]
                x_ref[j, 0, y, at] = field
                e_ref[j, 0, y, at] = left
        return c

    lax.fori_loop(0, cy // TILE, tile, 0)


def shards(nx, ny, adj, sig, elec):
    cx, cy, cz = sig.shape
    current = math.sqrt(nx * cx * ny * cy * cz)
    block = jax.ShapeDtypeStruct(adj.shape, jnp.float32)
    hbm = pl.BlockSpec(memory_space=pl.ANY)
    vmem = pl.BlockSpec(memory_space=pltpu.VMEM)
    padded = (cx + 2, cy + 2 * TILE, cz)
    dma = pltpu.SemaphoreType.DMA
    r, q, w, sums = pl.pallas_call(
        functools.partial(operator_kernel, nx, ny, current),
        out_shape=(block, block, block, jax.ShapeDtypeStruct((4 * NP, LANES), jnp.float32)),
        in_specs=[hbm, hbm, pl.BlockSpec(memory_space=pltpu.SMEM)],
        out_specs=(hbm, hbm, hbm, vmem),
        scratch_shapes=[
            pltpu.VMEM((F,) + padded, jnp.float32),
            pltpu.VMEM((F,) + padded, jnp.float32),
            pltpu.VMEM((F, cx, cy, cz), jnp.float32),
            pltpu.VMEM(padded, jnp.float32),
            pltpu.VMEM((7, cx, cy, cz), jnp.float32),
            pltpu.VMEM((4, F + 1, cx, cz), jnp.float32),
            pltpu.VMEM((4, F + 1, cx, cz), jnp.float32),
            pltpu.VMEM((4 * NP, TILE, LANES), jnp.float32),
            pltpu.VMEM((nx, 4 * NP, LANES), jnp.float32),
            pltpu.VMEM((ny, 4 * NP, LANES), jnp.float32),
            dma((5,)), dma((6,)), dma((6,)), dma((4,)), dma((4,)),
            dma((max(nx - 1, 1),)), dma((max(nx - 1, 1),)),
            dma((max(ny - 1, 1),)), dma((max(ny - 1, 1),)),
        ],
        compiler_params=pltpu.CompilerParams(collective_id=0, has_side_effects=True),
    )(adj, sig, elec)
    slab = pl.BlockSpec((F, 1, cy, cz), lambda x: (0, x, 0, 0))
    return pl.pallas_call(
        finish_kernel,
        grid=(cx,),
        out_shape=(block, block),
        in_specs=[pl.BlockSpec((4 * NP, LANES), lambda x: (0, 0)), slab, slab, slab],
        out_specs=(slab, slab),
        scratch_shapes=[pltpu.VMEM((2 * F * F, LANES), jnp.float32)],
    )(sums, r, q, w)


def solution(mesh):
    placed = (P(None, "gx", "gy", None), P("gx", "gy", None), P())
    return jax.shard_map(
        functools.partial(shards, mesh.shape["gx"], mesh.shape["gy"]),
        mesh=mesh,
        in_specs=placed,
        out_specs=(P(None, "gx", "gy", None), P(None, "gx", "gy", None)),
        check_vma=False,
    )
```

time: 345 us -> 55.8 us (0.16); the launches traced: 340 us -> 55.5 us
  matrix products: 135 us -> 0 us
  blocking collectives: 83.3 us -> 0 us
  Pallas kernels: 0 us -> 54.9 us
  other arithmetic: 52.9 us -> 0 us
  starting transfers between devices: 33.6 us -> 0 us
  local copies, waits for them, and re-layouts: 30.9 us -> 0 us
    dot_general x12 -> x0, matrix products: 134 us -> none  [the longest x4 73.6 us: gram(): jnp.einsum('ixyz,jxyz->ij', left, right, precision=lax.Precision.HIGHEST)]
    psum x2 -> x0, blocking collectives: 83.3 us -> none  [paired_products(): lax.psum((gram(residual, residual), gram(residual, image)), ('gx', 'gy'))]
    pallas_call x0 -> x2, Pallas kernels: none -> 54.9 us  [the longest x1 42.7 us: shards(): pl.pallas_call(functools.partial(operator_kernel, nx, ny, current), out_s...]
    ppermute x12 -> x0, starting transfers between devices: 33.6 us -> none  [the longest x6 25.8 us: with_halo(): lax.ppermute(lax.slice_in_dim(block, block.shape[dim] - width, None, axis...]
    concatenate x5 -> x0, other arithmetic: 24.3 us -> none  [with_halo(): block = jnp.concatenate([low, block, high], axis=dim)]
    add x5 -> x0, other arithmetic: 20.5 us -> none  [the longest x2 20.2 us: apply_operator(): total = total + coeff[None] * (center - other)]
    unnamed x38 -> x0, local copies, waits for them, and re-layouts: 19.1 us -> none
    scatter-add x1 -> x0, local copies, waits for them, and re-layouts: 8.89 us -> none  [shards(): right_side = adjoint_source.at[:, :, :, 0].add(spike)]
  transfers between devices with their start and end apart: 12 -> 0, of which waited for: 2 -> 0; matrix products, arithmetic and copies ran while one was open for 17% -> 0% of each run, Pallas kernels for 0% -> 0%
where the time goes in v1:
time: 55.8 us; the launch traced here: 55.5 us
  Pallas kernels  54.9 us (98%)
  between operations  0.64 us (1%)
    pallas_call x1, Pallas kernels, shards(): pl.pallas_call(functools.partial(operator_kernel, nx, ny, current), out_s...  42.7 us
    pallas_call x1, Pallas kernels, shards(): pl.pallas_call(finish_kernel, grid=(cx,), out_shape=(block, block), in_sp...  12.2 us

profile of v1, /device:TPU:0, one launch (start us, length us, event | category | flops | bytes accessed | tf_op | source)
XLA Modules:
  0.0 55.5 jit_solution(189325540246468541)
XLA Ops:
  0.6 42.7 %shard_map.50 = (f32[4,8,64,512]{3,2,1,0:T(8,128)}, f32[4,8,64,512]{3,2,1,0:T(8,128)}, f32[4,8,64,512]{3,2,1,0:T(8,128)}, f32[40,128]{1,0:T(8,128)}) custom-call(f32[4,8,64,512]{3,2,1,0:T(8,128)} %adj.1, f32[8,64,512]{2,1,0:T(8,128)} %sig.1, s32[4]{0:T(128)} %elec.1), custom_call_target="tpu_custom_call" | custom-call | tf_op jit(solution)/shard_map/pallas_call | solution.py:460
  43.4 12.2 %shard_map.51 = (f32[4,8,64,512]{3,2,1,0:T(8,128)}, f32[4,8,64,512]{3,2,1,0:T(8,128)}) custom-call(f32[40,128]{1,0:T(8,128)} %get-tuple-element.6.sums, f32[4,8,64,512]{3,2,1,0:T(8,128)} %get-tuple-element.7.r_ref, f32[4,8,64,512]{3,2,1,0:T(8,128)} %get-tuple-element.8.q_ref, f32[4,8,64,512]{3,2,1,0:T(8,128)} %get-tuple-element.9.w_ref), custom_call_target="tpu_custom_call" | custom-call | tf_op jit(solution)/shard_map/pallas_call | solution.py:483

commit v2 on v1

--- a/solution.py
+++ b/solution.py
@@ -13,6 +13,8 @@
 PAIRS = [(i, j) for i in range(F) for j in range(i, F)]
 NP = len(PAIRS)
 TILE = 8
+GRANT_A = 15 * 1024 * 1024
+GRANT_B = 5 * 1024 * 1024
 LANES = 128
 
 
@@ -24,8 +26,8 @@
 
 
 def operator_kernel(
-    nx, ny, current, adj, sig, elec, r_out, q_out, w_out, sums,
-    R, Q, W, S, wt, edge, got, acc, part_x, part_y,
+    nx, ny, current, adj, sig, elec, R, Q, W, sums,
+    S, wt, edge, got, acc, part_x, part_y,
     local, xs, xr, ys, yr, ax_s, ax_r, ay_s, ay_r,
 ):
     cx, cy, cz = sig.shape
@@ -141,9 +143,6 @@
     @pl.when(y_lo)
     def _():
         y_dn.start()
-
-    keep_r = pltpu.make_async_copy(R.at[:, pl.ds(1, cx), rows, :], r_out, local.at[2])
-    keep_r.start()
 
     @pl.when(y_lo)
     def _():
@@ -273,9 +272,6 @@
     def _():
         y_dn_q.start()
 
-    keep_q = pltpu.make_async_copy(Q.at[:, pl.ds(1, cx), rows, :], q_out, local.at[3])
-    keep_q.start()
-
     @pl.when(y_lo)
     def _():
         y_up_q.wait_recv()
@@ -302,8 +298,6 @@
         dn_q.wait_recv()
 
     lax.fori_loop(0, 2, ends(lambda k: second_plane(1 + k * (cx - 1))), 0)
-    keep_w = pltpu.make_async_copy(W, w_out, local.at[4])
-    keep_w.start()
 
     part_x[mx] = jnp.sum(acc[...], axis=1)
 
@@ -353,10 +347,6 @@
     def _():
         y_dn.wait_send()
         y_dn_q.wait_send()
-
-    keep_r.wait()
-    keep_q.wait()
-    keep_w.wait()
 
 
 def mat(a, b):
@@ -425,17 +415,19 @@
                 coef[pl.ds(i * F + j, 1), :] = m1[i][j]
                 coef[pl.ds(F * F + i * F + j, 1), :] = m2[i][j]
 
-    cy, cz = r_ref.shape[2:]
+    x = pl.program_id(0)
+    cy, cz = w_ref.shape[2:]
     c1 = [[jnp.broadcast_to(coef[pl.ds(i * F + j, 1), :], (TILE, LANES)) for j in range(F)] for i in range(F)]
     c2 = [[jnp.broadcast_to(coef[pl.ds(F * F + i * F + j, 1), :], (TILE, LANES)) for j in range(F)] for i in range(F)]
 
     def tile(t, c):
         y = pl.ds(pl.multiple_of(t * TILE, TILE), TILE)
+        wide_y = pl.ds(pl.multiple_of(t * TILE + TILE, TILE), TILE)
         for z in range(0, cz, LANES):
             at = pl.ds(z, LANES)
-            rs = [r_ref[f, 0, y, at] for f in range(F)]
-            qs = [q_ref[f, 0, y, at] for f in range(F)]
-            ws = [w_ref[f, 0, y, at] for f in range(F)]
+            rs = [r_ref[f, x + 1, wide_y, at] for f in range(F)]
+            qs = [q_ref[f, x + 1, wide_y, at] for f in range(F)]
+            ws = [w_ref[f, x, y, at] for f in range(F)]
             for j in range(F):
                 field = rs[0] * c1[0][j] - qs[0] * c2[0][j]
                 left = rs[j] - qs[0] * c1[0][j] + ws[0] * c2[0][j]
@@ -453,19 +445,19 @@
     cx, cy, cz = sig.shape
     current = math.sqrt(nx * cx * ny * cy * cz)
     block = jax.ShapeDtypeStruct(adj.shape, jnp.float32)
-    hbm = pl.BlockSpec(memory_space=pl.ANY)
+    hbm = pl.BlockSpec(memory_space=pltpu.HBM)
     vmem = pl.BlockSpec(memory_space=pltpu.VMEM)
     padded = (cx + 2, cy + 2 * TILE, cz)
+    wide = jax.ShapeDtypeStruct((F,) + padded, jnp.float32)
     dma = pltpu.SemaphoreType.DMA
+    adj = pltpu.with_memory_space_constraint(adj, pltpu.HBM)
+    sig = pltpu.with_memory_space_constraint(sig, pltpu.HBM)
     r, q, w, sums = pl.pallas_call(
         functools.partial(operator_kernel, nx, ny, current),
-        out_shape=(block, block, block, jax.ShapeDtypeStruct((4 * NP, LANES), jnp.float32)),
+        out_shape=(wide, wide, block, jax.ShapeDtypeStruct((4 * NP, LANES), jnp.float32)),
         in_specs=[hbm, hbm, pl.BlockSpec(memory_space=pltpu.SMEM)],
-        out_specs=(hbm, hbm, hbm, vmem),
+        out_specs=(vmem, vmem, vmem, vmem),
         scratch_shapes=[
-            pltpu.VMEM((F,) + padded, jnp.float32),
-            pltpu.VMEM((F,) + padded, jnp.float32),
-            pltpu.VMEM((F, cx, cy, cz), jnp.float32),
             pltpu.VMEM(padded, jnp.float32),
             pltpu.VMEM((7, cx, cy, cz), jnp.float32),
             pltpu.VMEM((4, F + 1, cx, cz), jnp.float32),
@@ -473,20 +465,21 @@
             pltpu.VMEM((4 * NP, TILE, LANES), jnp.float32),
             pltpu.VMEM((nx, 4 * NP, LANES), jnp.float32),
             pltpu.VMEM((ny, 4 * NP, LANES), jnp.float32),
-            dma((5,)), dma((6,)), dma((6,)), dma((4,)), dma((4,)),
+            dma((2,)), dma((6,)), dma((6,)), dma((4,)), dma((4,)),
             dma((max(nx - 1, 1),)), dma((max(nx - 1, 1),)),
             dma((max(ny - 1, 1),)), dma((max(ny - 1, 1),)),
         ],
-        compiler_params=pltpu.CompilerParams(collective_id=0, has_side_effects=True),
+        compiler_params=pltpu.CompilerParams(collective_id=0, has_side_effects=True, vmem_limit_bytes=GRANT_A),
     )(adj, sig, elec)
     slab = pl.BlockSpec((F, 1, cy, cz), lambda x: (0, x, 0, 0))
     return pl.pallas_call(
         finish_kernel,
         grid=(cx,),
         out_shape=(block, block),
-        in_specs=[pl.BlockSpec((4 * NP, LANES), lambda x: (0, 0)), slab, slab, slab],
+        in_specs=[vmem, vmem, vmem, vmem],
         out_specs=(slab, slab),
         scratch_shapes=[pltpu.VMEM((2 * F * F, LANES), jnp.float32)],
+        compiler_params=pltpu.CompilerParams(vmem_limit_bytes=GRANT_B),
     )(sums, r, q, w)
 
 

time: 55.8 us -> 50.9 us (0.912)
  Pallas kernels: 54.9 us -> 49.5 us
  local copies, waits for them, and re-layouts: 0 us -> 0.65 us
    pallas_call x1, Pallas kernels: 12.2 us -> 7.39 us  [shards(): pl.pallas_call(finish_kernel, grid=(cx,), out_shape=(block, block), in_sp...]
    unnamed x0 -> x2, local copies, waits for them, and re-layouts: none -> 0.65 us
    pallas_call x1, Pallas kernels: 42.7 us -> 42.1 us  [shards(): pl.pallas_call(functools.partial(operator_kernel, nx, ny, current), out_s...]
where the time goes in v2:
time: 50.9 us; the launch traced here: 50.8 us
  Pallas kernels  49.5 us (97%)
  local copies, waits for them, and re-layouts  0.65 us (1%)
  between operations  0.65 us (1%)
    pallas_call x1, Pallas kernels, shards(): pl.pallas_call(functools.partial(operator_kernel, nx, ny, current), out_s...  42.1 us
    pallas_call x1, Pallas kernels, shards(): pl.pallas_call(finish_kernel, grid=(cx,), out_shape=(block, block), in_sp...  7.39 us

profile of v2, /device:TPU:0, one launch (start us, length us, event | category | flops | bytes accessed | tf_op | source)
XLA Modules:
  0.0 50.8 jit_solution(11639175689932945219)
XLA Ops:
  0.6 0.0 copy-start
  0.6 0.6 %copy-done = s32[4]{0:T(128)S(1)} copy-done((s32[4]{0:T(128)S(1)}, s32[4]{0:T(128)}, u32[]{:S(2)}) %copy-start) | copy-done | bytes 40
  1.3 42.1 %shard_map.50 = (f32[4,10,80,512]{3,2,1,0:T(8,128)S(1)}, f32[4,10,80,512]{3,2,1,0:T(8,128)S(1)}, f32[4,8,64,512]{3,2,1,0:T(8,128)S(1)}, f32[40,128]{1,0:T(8,128)S(1)}) custom-call(f32[4,8,64,512]{3,2,1,0:T(8,128)} %adj.1, f32[8,64,512]{2,1,0:T(8,128)} %sig.1, s32[4]{0:T(128)S(1)} %copy-done), custom_call_target="tpu_custom_call" | custom-call | tf_op jit(solution)/shard_map/pallas_call | solution.py:455
  43.4 7.4 %shard_map.51 = (f32[4,8,64,512]{3,2,1,0:T(8,128)}, f32[4,8,64,512]{3,2,1,0:T(8,128)}) custom-call(f32[40,128]{1,0:T(8,128)S(1)} %get-tuple-element.6.sums, f32[4,10,80,512]{3,2,1,0:T(8,128)S(1)} %get-tuple-element.7.r_ref, f32[4,10,80,512]{3,2,1,0:T(8,128)S(1)} %get-tuple-element.8.q_ref, f32[4,8,64,512]{3,2,1,0:T(8,128)S(1)} %get-tuple-element.9.w_ref), custom_call_target="tpu_custom_call" | custom-call | tf_op jit(solution)/shard_map/pallas_call | solution.py:475
Async XLA Ops:
  0.6 0.7 %copy-start = (s32[4]{0:T(128)S(1)}, s32[4]{0:T(128)}, u32[]{:S(2)}) copy-start(s32[4]{0:T(128)} %elec.1) | copy-start | bytes 52

commit v3 on v2

--- a/solution.py
+++ b/solution.py
@@ -54,10 +54,13 @@
 
     up_s = remote(sig.at[cx - 1], S.at[0, rows, :], xs.at[0], xr.at[0], "gx", above)
     dn_s = remote(sig.at[0], S.at[cx + 1, rows, :], xs.at[1], xr.at[1], "gx", below)
-    up_r = remote(adj.at[:, cx - 1], R.at[:, 0, rows, :], xs.at[2], xr.at[2], "gx", above)
-    dn_r = remote(adj.at[:, 0], R.at[:, cx + 1, rows, :], xs.at[3], xr.at[3], "gx", below)
-    up_q = remote(Q.at[:, cx, rows, :], Q.at[:, 0, rows, :], xs.at[4], xr.at[4], "gx", above)
-    dn_q = remote(Q.at[:, 1, rows, :], Q.at[:, cx + 1, rows, :], xs.at[5], xr.at[5], "gx", below)
+    up_r, dn_r, up_q, dn_q = [], [], [], []
+    for f in range(F):
+        a = 2 + 4 * f
+        up_r.append(remote(adj.at[f, cx - 1], R.at[f, 0, rows, :], xs.at[a], xr.at[a], "gx", above))
+        dn_r.append(remote(adj.at[f, 0], R.at[f, cx + 1, rows, :], xs.at[a + 1], xr.at[a + 1], "gx", below))
+        up_q.append(remote(Q.at[f, cx, rows, :], Q.at[f, 0, rows, :], xs.at[a + 2], xr.at[a + 2], "gx", above))
+        dn_q.append(remote(Q.at[f, 1, rows, :], Q.at[f, cx + 1, rows, :], xs.at[a + 3], xr.at[a + 3], "gx", below))
     y_up = remote(edge.at[0], got.at[0], ys.at[0], yr.at[0], "gy", right)
     y_dn = remote(edge.at[1], got.at[1], ys.at[1], yr.at[1], "gy", left)
     y_up_q = remote(edge.at[2, pl.ds(0, F)], got.at[2, pl.ds(0, F)], ys.at[2], yr.at[2], "gy", right)
@@ -66,12 +69,14 @@
     @pl.when(has_hi)
     def _():
         up_s.start()
-        up_r.start()
+        for copy in up_r:
+            copy.start()
 
     @pl.when(has_lo)
     def _():
         dn_s.start()
-        dn_r.start()
+        for copy in dn_r:
+            copy.start()
 
     acc[...] = jnp.zeros_like(acc)
     edge_plane = jnp.zeros((cy, cz), jnp.float32)
@@ -103,9 +108,9 @@
     row_id = lax.broadcasted_iota(jnp.int32, (cy, LANES), 0)
     first = lax.broadcasted_iota(jnp.int32, (cy, LANES), 1) == 0
 
-    def spike(x):
+    def spike(x, fields=range(F)):
         cell = row_id + ((mx * cx + x - 1) * total_y + my * cy)
-        for f in range(F):
+        for f in fields:
             here = jnp.where(first & (cell == elec[f]), current, 0.0)
             R[f, x, rows, pl.ds(0, LANES)] = R[f, x, rows, pl.ds(0, LANES)] + here
 
@@ -183,34 +188,57 @@
         out = out - zp * pltpu.roll(mid, cz - 1, axis=1)
         return mid, out
 
+    def tile_weights(x, t):
+        y = TILE + t * TILE
+        here = S[x, pl.ds(y, TILE), :]
+        others = (
+            S[x - 1, pl.ds(y, TILE), :],
+            S[x + 1, pl.ds(y, TILE), :],
+            S[x, pl.ds(y - 1, TILE), :],
+            S[x, pl.ds(y + 1, TILE), :],
+            jnp.where(lane == 0, 0.0, pltpu.roll(here, 1, axis=1)),
+            jnp.where(lane == cz - 1, 0.0, pltpu.roll(here, cz - 1, axis=1)),
+        )
+        diag = jnp.zeros_like(here)
+        weights = []
+        for other in others:
+            inside = other > 0.0
+            mean = 0.5 * (here + other)
+            diag = diag + jnp.where(inside, mean, here)
+            weights.append(jnp.where(inside, mean, 0.0))
+        weights = [diag] + weights
+        for k in range(7):
+            wt[k, x - 1, pl.ds(t * TILE, TILE), :] = weights[k]
+        return weights
+
     def first_plane(x):
         for t in range(cy // TILE):
             y = TILE + t * TILE
-            here = S[x, pl.ds(y, TILE), :]
-            others = (
-                S[x - 1, pl.ds(y, TILE), :],
-                S[x + 1, pl.ds(y, TILE), :],
-                S[x, pl.ds(y - 1, TILE), :],
-                S[x, pl.ds(y + 1, TILE), :],
-                jnp.where(lane == 0, 0.0, pltpu.roll(here, 1, axis=1)),
-                jnp.where(lane == cz - 1, 0.0, pltpu.roll(here, cz - 1, axis=1)),
-            )
-            diag = jnp.zeros_like(here)
-            weights = []
-            for other in others:
-                inside = other > 0.0
-                mean = 0.5 * (here + other)
-                diag = diag + jnp.where(inside, mean, here)
-                weights.append(jnp.where(inside, mean, 0.0))
-            weights = [diag] + weights
-            for k in range(7):
-                wt[k, x - 1, pl.ds(t * TILE, TILE), :] = weights[k]
+            weights = tile_weights(x, t)
             rs, qs = [], []
             for f in range(F):
                 mid, out = apply(R, f, x, y, weights)
                 Q[f, x, pl.ds(y, TILE), :] = out
                 rs.append(mid)
                 qs.append(out)
+            add_grams(0, rs, rs)
+            add_grams(NP, rs, qs)
+
+    def edge_weights(x):
+        for t in range(cy // TILE):
+            tile_weights(x, t)
+
+    def edge_field(x, f):
+        for t in range(cy // TILE):
+            y = TILE + t * TILE
+            weights = [wt[k, x - 1, pl.ds(t * TILE, TILE), :] for k in range(7)]
+            Q[f, x, pl.ds(y, TILE), :] = apply(R, f, x, y, weights)[1]
+
+    def edge_grams(x):
+        for t in range(cy // TILE):
+            y = TILE + t * TILE
+            rs = [R[f, x, pl.ds(y, TILE), :] for f in range(F)]
+            qs = [Q[f, x, pl.ds(y, TILE), :] for f in range(F)]
             add_grams(0, rs, rs)
             add_grams(NP, rs, qs)
 
@@ -235,32 +263,41 @@
 
     lax.fori_loop(2, cx, run(first_plane), 0)
 
-    @pl.when(has_lo)
-    def _():
-        up_s.wait_recv()
-        up_r.wait_recv()
-
-    @pl.when(has_hi)
-    def _():
-        dn_s.wait_recv()
-        dn_r.wait_recv()
-
     def ends(plane):
         def one(k, c):
             plane(k)
             return c
         return one
 
-    lax.fori_loop(0, 2, ends(lambda k: spike(k * (cx + 1))), 0)
-    lax.fori_loop(0, 2, ends(lambda k: first_plane(1 + k * (cx - 1))), 0)
+    @pl.when(has_lo)
+    def _():
+        up_s.wait_recv()
 
     @pl.when(has_hi)
     def _():
-        up_q.start()
-
-    @pl.when(has_lo)
-    def _():
-        dn_q.start()
+        dn_s.wait_recv()
+
+    lax.fori_loop(0, 2, ends(lambda k: edge_weights(1 + k * (cx - 1))), 0)
+
+    for f in range(F):
+        @pl.when(has_lo)
+        def _():
+            up_r[f].wait_recv()
+
+        @pl.when(has_hi)
+        def _():
+            dn_r[f].wait_recv()
+
+        lax.fori_loop(0, 2, ends(lambda k: spike(k * (cx + 1), (f,))), 0)
+        lax.fori_loop(0, 2, ends(lambda k: edge_field(1 + k * (cx - 1), f)), 0)
+
+        @pl.when(has_hi)
+        def _():
+            up_q[f].start()
+
+        @pl.when(has_lo)
+        def _():
+            dn_q[f].start()
 
     pack(lambda x: [row_q(f, x) for f in range(F)], F, 2)
 
@@ -271,6 +308,8 @@
     @pl.when(y_lo)
     def _():
         y_dn_q.start()
+
+    lax.fori_loop(0, 2, ends(lambda k: edge_grams(1 + k * (cx - 1))), 0)
 
     @pl.when(y_lo)
     def _():
@@ -291,11 +330,13 @@
 
     @pl.when(has_lo)
     def _():
-        up_q.wait_recv()
+        for copy in up_q:
+            copy.wait_recv()
 
     @pl.when(has_hi)
     def _():
-        dn_q.wait_recv()
+        for copy in dn_q:
+            copy.wait_recv()
 
     lax.fori_loop(0, 2, ends(lambda k: second_plane(1 + k * (cx - 1))), 0)
 
@@ -329,14 +370,14 @@
     @pl.when(has_hi)
     def _():
         up_s.wait_send()
-        up_r.wait_send()
-        up_q.wait_send()
+        for copy in up_r + up_q:
+            copy.wait_send()
 
     @pl.when(has_lo)
     def _():
         dn_s.wait_send()
-        dn_r.wait_send()
-        dn_q.wait_send()
+        for copy in dn_r + dn_q:
+            copy.wait_send()
 
     @pl.when(y_hi)
     def _():
@@ -465,7 +506,7 @@
             pltpu.VMEM((4 * NP, TILE, LANES), jnp.float32),
             pltpu.VMEM((nx, 4 * NP, LANES), jnp.float32),
             pltpu.VMEM((ny, 4 * NP, LANES), jnp.float32),
-            dma((2,)), dma((6,)), dma((6,)), dma((4,)), dma((4,)),
+            dma((2,)), dma((2 + 4 * F,)), dma((2 + 4 * F,)), dma((4,)), dma((4,)),
             dma((max(nx - 1, 1),)), dma((max(nx - 1, 1),)),
             dma((max(ny - 1, 1),)), dma((max(ny - 1, 1),)),
         ],

time: 50.9 us -> 51.5 us (1.012)
    pallas_call x1, Pallas kernels: 42.1 us -> 42.7 us  [shards(): pl.pallas_call(functools.partial(operator_kernel, nx, ny, current), out_s...]
where the time goes in v3:
time: 51.5 us; the launch traced here: 51.3 us
  Pallas kernels  50 us (97%)
  local copies, waits for them, and re-layouts  0.65 us (1%)
  between operations  0.65 us (1%)
    pallas_call x1, Pallas kernels, shards(): pl.pallas_call(functools.partial(operator_kernel, nx, ny, current), out_s...  42.7 us
    pallas_call x1, Pallas kernels, shards(): pl.pallas_call(finish_kernel, grid=(cx,), out_shape=(block, block), in_sp...  7.39 us

profile of v3, /device:TPU:0, one launch (start us, length us, event | category | flops | bytes accessed | tf_op | source)
XLA Modules:
  0.0 51.3 jit_solution(16971452072472185015)
XLA Ops:
  0.6 0.0 copy-start
  0.6 0.6 %copy-done = s32[4]{0:T(128)S(1)} copy-done((s32[4]{0:T(128)S(1)}, s32[4]{0:T(128)}, u32[]{:S(2)}) %copy-start) | copy-done | bytes 40
  1.3 42.7 %shard_map.50 = (f32[4,10,80,512]{3,2,1,0:T(8,128)S(1)}, f32[4,10,80,512]{3,2,1,0:T(8,128)S(1)}, f32[4,8,64,512]{3,2,1,0:T(8,128)S(1)}, f32[40,128]{1,0:T(8,128)S(1)}) custom-call(f32[4,8,64,512]{3,2,1,0:T(8,128)} %adj.1, f32[8,64,512]{2,1,0:T(8,128)} %sig.1, s32[4]{0:T(128)S(1)} %copy-done), custom_call_target="tpu_custom_call" | custom-call | tf_op jit(solution)/shard_map/pallas_call | solution.py:496
  43.9 7.4 %shard_map.51 = (f32[4,8,64,512]{3,2,1,0:T(8,128)}, f32[4,8,64,512]{3,2,1,0:T(8,128)}) custom-call(f32[40,128]{1,0:T(8,128)S(1)} %get-tuple-element.6.sums, f32[4,10,80,512]{3,2,1,0:T(8,128)S(1)} %get-tuple-element.7.r_ref, f32[4,10,80,512]{3,2,1,0:T(8,128)S(1)} %get-tuple-element.8.q_ref, f32[4,8,64,512]{3,2,1,0:T(8,128)S(1)} %get-tuple-element.9.w_ref), custom_call_target="tpu_custom_call" | custom-call | tf_op jit(solution)/shard_map/pallas_call | solution.py:516
Async XLA Ops:
  0.6 0.7 %copy-start = (s32[4]{0:T(128)S(1)}, s32[4]{0:T(128)}, u32[]{:S(2)}) copy-start(s32[4]{0:T(128)} %elec.1) | copy-start | bytes 52
